TPU v7x, 512 devices: a whole 4x4x16 slice. The times are simulated.
512 devices in a mesh: ctx: 64 (over y, z), tp: 8 (over x, core).
Axes of the slice: x: 4, y: 4, z: 16, core: 2. Of those that a mesh axis runs over, the one named last changes fastest.
Arguments:
- query_rows: bfloat16 [32768, 4096], P('ctx', 'tp'), may hold values from -6 to 6
- key_rows: bfloat16 [32768, 4096], P('ctx', 'tp'), may hold values from -0.52734375 to 0.52734375
- value_rows: bfloat16 [32768, 4096], P('ctx', 'tp'), may hold values from -6 to 6
- log_decay: float32 [32, 32768], P('tp', 'ctx'), may hold values from -1 to 0
- norm_gain: float32 [4096], P('tp'), may hold values from 0.25 to 1.75
- out_weight: bfloat16 [4096, 3072], P(None, 'tp'), may hold values from -0.09375 to 0.09375
Outputs:
- projected: bfloat16 [32768, 3072], P('ctx', 'tp')
All inputs are finite; a program needn't handle non-finite values.
Results may differ from a plain program's by a relative error of at most 0.015.
Values may be sent and summed in bfloat16 or wider, within the bound.
A program may use at most 64 MiB of HBM per device.

v0:
```python
import jax
import jax.numpy as jnp
from jax import lax
from jax.sharding import PartitionSpec as P

HEADS = 32
HEAD_DIM = 128
BLOCK = 128


def entering_2(part, axis, combine, identity):
    place = lax.axis_index(axis)
    gathered = jax.tree.map(lambda a: lax.all_gather(a, axis), part)
    state = jax.tree.map(lambda a, e: jnp.zeros_like(a) + jnp.asarray(e, a.dtype), part, identity)

    def one(lap, state):
        return combine(
            state, jax.tree.map(lambda a: lax.dynamic_index_in_dim(a, lap, 0, False), gathered)
        )

    return lax.fori_loop(0, place, one, state)


def chain_combine(earlier, later):
    return (earlier[0] * later[0], later[0][:, None, None] * earlier[1] + later[1])


def incoming_from(shard_decay, shard_state):
    identity = (jnp.ones_like(shard_decay), jnp.zeros_like(shard_state))
    result = entering_2((shard_decay, shard_state), "ctx", chain_combine, identity)
    return result[1]


def split_parts(values):
    high = values.astype(jnp.bfloat16)
    low = (values - high.astype(jnp.float32)).astype(jnp.bfloat16)
    return (high, low)


def split_einsum(form, narrow, wide_first, wide_second):
    if narrow == 0:
        first = jnp.einsum(form, wide_first[0], wide_second, preferred_element_type=jnp.float32)
        second = jnp.einsum(form, wide_first[1], wide_second, preferred_element_type=jnp.float32)
    else:
        first = jnp.einsum(form, wide_first, wide_second[0], preferred_element_type=jnp.float32)
        second = jnp.einsum(form, wide_first, wide_second[1], preferred_element_type=jnp.float32)
    return first + second


def per_device(query_rows, key_rows, value_rows, log_decay, norm_gain, out_weight):
    length = query_rows.shape[0]
    feature_count = query_rows.shape[1]
    head_count = log_decay.shape[0]
    head_width = feature_count // head_count
    blocks = length // BLOCK
    q_block = query_rows.reshape(blocks, BLOCK, head_count, head_width)
    k_block = key_rows.reshape(blocks, BLOCK, head_count, head_width)
    v_block = value_rows.reshape(blocks, BLOCK, head_count, head_width)
    cum = jnp.cumsum(log_decay.reshape(head_count, blocks, BLOCK), axis=-1)
    causal = jnp.arange(BLOCK)[:, None] >= jnp.arange(BLOCK)[None, :]
    spread_log = cum[..., :, None] - cum[..., None, :]
    factor = jnp.where(causal, jnp.exp(jnp.where(causal, spread_log, 0.0)), 0.0)
    scores = jnp.einsum("bthe,bshe->hbts", q_block, k_block, preferred_element_type=jnp.float32)
    weights = (scores * factor).astype(jnp.bfloat16)
    inside_part = jnp.einsum(
        "hbts,bshe->bthe", weights, v_block, preferred_element_type=jnp.float32
    )
    to_end = jnp.transpose(jnp.exp(cum[..., -1:] - cum), (1, 2, 0))
    k_scaled = k_block.astype(jnp.float32) * to_end[..., None]
    block_states = split_einsum("bshe,bshf->bhef", 0, split_parts(k_scaled), v_block)
    block_totals = cum[..., -1]
    block_decay = jnp.exp(block_totals)
    offsets = jnp.cumsum(block_totals, axis=1) - block_totals
    running = jnp.zeros((head_count, head_width, head_width), jnp.float32)
    entering_list = []
    for index_block in range(blocks):
        entering_list.append(running)
        running = block_decay[:, index_block][:, None, None] * running + block_states[index_block]
    entering = jnp.stack(entering_list, axis=0)
    shard_decay = jnp.exp(jnp.sum(block_totals, axis=1))
    growth = jnp.transpose(jnp.exp(cum), (1, 2, 0))[..., None]
    incoming = incoming_from(shard_decay, running)
    entering_all = entering + jnp.transpose(jnp.exp(offsets))[:, :, None, None] * incoming[None]
    carried_part = split_einsum("bthe,bhef->bthf", 1, q_block, split_parts(entering_all)) * growth
    attention = inside_part + carried_part
    attention = attention.reshape(length, feature_count)
    squares = jnp.sum(attention * attention, axis=-1)
    summed = lax.psum(squares, "tp")
    scale = lax.rsqrt(summed / (HEADS * HEAD_DIM) + 1e-06)
    normed = (attention * scale[:, None] * norm_gain).astype(jnp.bfloat16)
    projected = jnp.dot(
        lax.all_gather(normed, "tp", axis=1, tiled=True),
        out_weight,
        preferred_element_type=jnp.float32,
    )
    return projected.astype(jnp.bfloat16)


def solution(mesh):
    in_specs = (
        P("ctx", "tp"),
        P("ctx", "tp"),
        P("ctx", "tp"),
        P("tp", "ctx"),
        P("tp"),
        P(None, "tp"),
    )
    out_specs = P("ctx", "tp")
    return jax.shard_map(
        per_device, mesh=mesh, in_specs=in_specs, out_specs=out_specs, check_vma=False
    )
```

profile of v0, /device:TPU:1, one launch (start us, length us, event | category | flops | bytes accessed | tf_op | source)
XLA Modules:
  0.0 353.3 jit_solution(14344379508308429635)
XLA Ops:
  6.5 0.9 reshape.42
  7.4 1.2 reduce_window_sum.24
  8.6 0.2 slice_reduce_fusion
  8.8 0.2 reduce_window_sum.26
  9.1 2.0 reshape.41
  11.0 2.1 copy.39
  13.1 2.0 reshape.43
  15.0 1.5 fusion.11
  16.5 1.5 convolution_add_fusion.1
  18.1 0.2 slice_reduce_fusion.2
  18.3 1.1 slice_add_fusion
  19.5 1.3 dynamic-slice
  21.3 0.1 exponential_dynamic-update-slice_fusion
  21.4 123.6 %all-reduce = f32[256]{0:T(256)S(1)} all-reduce(f32[256]{0:T(256)S(1)} %exponential_dynamic-update-slice_fusion), channel_id=2, replica_groups=mesh['ctx'=64,'tp'=8] {'ctx'}, use_global_device_ids=true, to_apply=%add | all-reduce | flops 256 | bytes 2048
  145.2 2.0 reshape.40
  147.2 3.1 convolution_bitcast_fusion
  150.3 68.3 %all-gather.4.cloned.1.call-done = f32[64,4,128,128]{3,2,1,0:T(8,128)} async-done(((f32[1,4,128,128]{3,2,1,0:T(8,128)}), f32[64,4,128,128]{3,2,1,0:T(8,128)}) %all-gather.4.cloned.1.call-update) | async-done | bytes 16777232 | tf_op jit(solution)/shard_map/all_gather | solution.py:13
  218.7 1.9 fusion.27
  220.6 3.3 multiply_reduce_fusion
  223.9 2.5 copy.49
  226.5 12.7 %psum.7 = f32[512]{0:T(512)S(1)} all-reduce(f32[512]{0:T(512)S(1)} %bitcast.40), channel_id=1, replica_groups=mesh['ctx'=64,'tp'=8] {'tp'}, use_global_device_ids=true, to_apply=%region_6.7 | all-reduce | flops 512 | bytes 4096 | tf_op jit(solution)/shard_map/psum | solution.py:88
  239.2 2.2 fusion.5
  241.4 99.7 %all-gather.6.cloned.1.call-done = bf16[512,4096]{1,0:T(8,128)(2,1)} async-done(((bf16[512,512]{1,0:T(8,128)(2,1)}), bf16[512,4096]{1,0:T(8,128)(2,1)}) %all-gather.6.cloned.1.call-update) | async-done | bytes 4194320 | tf_op jit(solution)/shard_map/all_gather | solution.py:92
  341.2 5.3 %convolution_convert_fusion = bf16[512,384]{1,0:T(8,128)(2,1)} fusion(bf16[512,4096]{1,0:T(8,128)(2,1)} %all-gather.6.cloned.1.call-done, bf16[4096,384]{1,0:T(8,128)(2,1)S(1)} %copy-done), kind=kOutput, calls=%fused_computation.10 | convolution fusion | flops 1610809344 | bytes 7733248 | tf_op jit(solution)/shard_map/dot_general | solution.py:91
  (21 shorter events, 0.4 us)
Async XLA Ops:
  6.5 334.6 %copy-start = (bf16[4096,384]{1,0:T(8,128)(2,1)S(1)}, bf16[4096,384]{1,0:T(8,128)(2,1)}, u32[]{:S(2)}) copy-start(bf16[4096,384]{1,0:T(8,128)(2,1)} %param.13) | copy-start | bytes 9437188
  6.5 212.1 %all-gather.4.cloned.1.call-start = ((), (), s32[]{:S(2)}) async-start(), calls=%async_computation | async-start | bytes 17039360 | tf_op jit(solution)/shard_map/all_gather | solution.py:13
  19.4 321.8 %all-gather.6.cloned.1.call-start = ((), (), s32[]{:S(2)}) async-start(), calls=%async_computation.1 | async-start | bytes 4718592 | tf_op jit(solution)/shard_map/all_gather | solution.py:92
  218.7 20.6 %copy-start.1 = (f32[512]{0:T(512)S(1)}, f32[512]{0:T(512)}, u32[]{:S(2)}) copy-start(f32[512]{0:T(512)} %param.12) | copy-start | bytes 6148
Sparse Core Ops, SparseCore 0:
  19.5 199.0 all-gather.3
  241.6 99.5 all-gather.5
where the time goes:
time: 356 us; the launch traced here: 353 us
  waiting for transfers between devices  168 us (47%)
  blocking collectives  136 us (38%)
  matrix products  16.6 us (5%)
  between operations  14.1 us (4%)
  local copies, waits for them, and re-layouts  13 us (4%)
  other arithmetic  5.13 us (1%)
    unnamed x1, blocking collectives  124 us
    all_gather x1, waiting for transfers between devices, per_device(): lax.all_gather(normed, 'tp', axis=1, tiled=True)  99.7 us
    all_gather x1, waiting for transfers between devices, entering_2(): gathered = jax.tree.map(lambda a: lax.all_gather(a, axis), part)  68.3 us
    psum x1, blocking collectives, per_device(): summed = lax.psum(squares, 'tp')  12.7 us
  transfers between devices with their start and end apart: 2, of which 2 were waited for; matrix products, arithmetic and copies ran while one was open for 2% of the time, Pallas kernels for 0%

commit v1 on v0

--- a/solution.py
+++ b/solution.py
@@ -89,7 +89,9 @@
     scale = lax.rsqrt(summed / (HEADS * HEAD_DIM) + 1e-06)
     normed = (attention * scale[:, None] * norm_gain).astype(jnp.bfloat16)
     projected = jnp.dot(
-        lax.all_gather(normed, "tp", axis=1, tiled=True),
+        jnp.concatenate(
+            lax.all_to_all(jnp.stack([normed] * lax.axis_size("tp")), "tp", 0, 0), axis=1
+        ),
         out_weight,
         preferred_element_type=jnp.float32,
     )

time: 356 us -> 371 us (1.042)
  the two profiles are of different devices: /device:TPU:1 before, /device:TPU:504 now
where the time goes in v1:
time: 371 us; the launch traced here: 368 us
  blocking collectives  206 us (56%)
  other arithmetic  72 us (19%)
  waiting for transfers between devices  42.4 us (11%)
  local copies, waits for them, and re-layouts  17.2 us (5%)
  matrix products  14.4 us (4%)
  between operations  14.1 us (4%)
    unnamed x1, blocking collectives  139 us
    add x63, other arithmetic, chain_combine(): later[0][:, None, None] * earlier[1] + later[1]  66.9 us
    all_to_all x1, blocking collectives, per_device(): lax.all_to_all(jnp.stack([normed] * lax.axis_size('tp')), 'tp', 0, 0)  52.8 us
    all_gather x1, waiting for transfers between devices, entering_2(): gathered = jax.tree.map(lambda a: lax.all_gather(a, axis), part)  42.4 us
    psum x1, blocking collectives, per_device(): summed = lax.psum(squares, 'tp')  14.4 us
  transfers between devices with their start and end apart: 1, of which 1 were waited for; matrix products, arithmetic and copies ran while one was open for 2% of the time, Pallas kernels for 0%

profile of v1, /device:TPU:504, one launch (start us, length us, event | category | flops | bytes accessed | tf_op | source)
XLA Modules:
  0.0 368.4 jit_solution(3828141726856711832)
XLA Ops:
  7.4 1.2 reduce_window_sum.24
  9.1 2.0 reshape.65
  11.0 2.1 copy.40
  13.1 2.0 reshape.67
  15.0 1.5 fusion.11
  16.5 1.5 convolution_add_fusion.1
  18.3 1.1 slice_add_fusion
  19.4 1.3 dynamic-slice
  21.4 138.9 %all-reduce = f32[256]{0:T(256)S(1)} all-reduce(f32[256]{0:T(256)S(1)} %exponential_dynamic-update-slice_fusion), channel_id=2, replica_groups=mesh['ctx'=64,'tp'=8] {'ctx'}, use_global_device_ids=true, to_apply=%add | all-reduce | flops 256 | bytes 2048
  160.5 2.0 reshape.64
  162.5 3.1 convolution_bitcast_fusion
  165.6 42.4 %all-gather.3.cloned.1.call-done = f32[64,4,128,128]{3,2,1,0:T(8,128)} async-done(((f32[1,4,128,128]{3,2,1,0:T(8,128)}), f32[64,4,128,128]{3,2,1,0:T(8,128)}) %all-gather.3.cloned.1.call-update) | async-done | bytes 16777232 | tf_op jit(solution)/shard_map/all_gather | solution.py:13
  208.0 69.8 %while.12 = (s32[]{:T(128)}, f32[4,128,128]{2,1,0:T(8,128)S(1)}, s32[]{:T(128)}, f32[64,4]{1,0:T(8,128)S(1)}, f32[64,4,128,128]{3,2,1,0:T(8,128)}, /*index=5*/s32[]{:T(128)}, s32[]{:T(128)}, s32[]{:T(128)}) while((s32[]{:T(128)}, f32[4,128,128]{2,1,0:T(8,128)S(1)}, s32[]{:T(128)}, f32[64,4]{1,0:T(8,128)S(1)}, f32[64,4,128,128]{3,2,1,0:T(8,128)}, ...), condition=%wide.region_4.5_spmd, body=%wide.region_3.4_spmd.sunk | while | flops 131077 | bytes 786607 | solution.py:21
  208.0 1.1 bitcast_add_fusion.2
  209.1 1.1 bitcast_add_fusion.2
  277.8 1.9 fusion.27
  279.8 3.3 multiply_reduce_fusion
  283.1 2.5 copy.50
  285.6 14.4 %psum.7 = f32[512]{0:T(512)S(1)} all-reduce(f32[512]{0:T(512)S(1)} %bitcast.44), channel_id=1, replica_groups=mesh['ctx'=64,'tp'=8] {'tp'}, use_global_device_ids=true, to_apply=%region_6.7 | all-reduce | flops 512 | bytes 4096 | tf_op jit(solution)/shard_map/psum | solution.py:88
  300.0 2.2 fusion.5
  302.2 2.0 copy.51
  304.3 1.4 stack.5
  305.7 52.8 %all_to_all.5 = bf16[8,512,512]{1,2,0:T(8,128)(2,1)S(1)} all-to-all(bf16[8,512,512]{1,2,0:T(8,128)(2,1)S(1)} %stack.5), channel_id=1, replica_groups=mesh['ctx'=64,'tp'=8] {'tp'}, dimensions={0} | all-to-all | bytes 8388608 | tf_op jit(solution)/shard_map/all_to_all | solution.py:93
  358.5 3.1 convolution_convert_fusion
  (147 shorter events, 67.4 us)
Async XLA Ops:
  6.5 351.9 %copy-start = (bf16[4096,384]{1,0:T(8,128)(2,1)S(1)}, bf16[4096,384]{1,0:T(8,128)(2,1)}, u32[]{:S(2)}) copy-start(bf16[4096,384]{1,0:T(8,128)(2,1)} %param.13) | copy-start | bytes 9437188
  6.5 201.4 %all-gather.3.cloned.1.call-start = ((), (), s32[]{:S(2)}) async-start(), calls=%async_computation.1 | async-start | bytes 17039360 | tf_op jit(solution)/shard_map/all_gather | solution.py:13
  277.8 22.2 %copy-start.1 = (f32[512]{0:T(512)S(1)}, f32[512]{0:T(512)}, u32[]{:S(2)}) copy-start(f32[512]{0:T(512)} %param.12) | copy-start | bytes 6148
Sparse Core Ops, SparseCore 0:
  19.5 188.4 all-gather.2
